TPU v7x, 32 devices: a whole 2x2x4 slice. The times are simulated.
32 devices in a mesh: groups: 2 (over x), psg: 16 (over z, y, core).
Axes of the slice: x: 2, y: 2, z: 4, core: 2. Of those that a mesh axis runs over, the one named last changes fastest.
Arguments:
- queries: bfloat16 [64, 32, 128], P(('groups', 'psg')), parts along dimension 0, may hold values from -0.29882812 to 0.29882812
- candidates: int32 [64, 512], P(('groups', 'psg')), parts along dimension 0, may hold values from 0 to 159
- centroids: bfloat16 [8192, 128], P('psg'), may hold values from -6 to 6
- bucket_weights: float32 [4, 128], replicated, may hold values from -1 to 1
- centroid_shard: int32 [32768, 1], P('psg'), may hold values from 0 to 15; in each aligned block of 2048 rows (0 to 2047, 2048 to 4095, ...) at most 256 rows name the same one
- centroid_row: int32 [32768], P('psg'), may hold values from 0 to 511
- residual_codes: int32 [32768, 128], P('psg'), may hold values from 0 to 3
- tile_count: int32 [160], replicated, may hold values from 1 to 3, 256 in all
- last_fill: int32 [160], replicated, may hold values from 1 to 128
Outputs:
- scores: float32 [64, 512], P(('groups', 'psg')), parts along dimension 0
There are 2 independent parts, one for each index of `groups`. A program takes and returns all parts, laid end to end along the dimension named above; an argument that names none is the same for every part. Nothing has to cross between parts.
Inputs may be any that keep to these rules, and one draw needn't show every extreme that they name: `tile_count`: tiles are numbered along psg, device k holding tiles k * 16 onward; the counts sum to 256, so a passage may continue on the next device. `centroid_shard`: among the 2048 token slots of one device, at most 256 name the same device; on some device some value is named exactly 256 times.
All inputs are finite; a program needn't handle non-finite values.
Results may differ from a plain program's by a relative error of at most 0.0003.
Values may be sent and summed in bfloat16 or wider, within the bound.
No kernel may reach another device: no remote copies, remote signals or barrier semaphores. Data moves between devices by JAX's collectives and lax.ppermute only.
A program may use at most 64 MiB of HBM per device.

v0:
```python
import jax
import jax.numpy as jnp
from jax import lax
from jax.sharding import PartitionSpec as P

TILE = 128
epsilon = 1e-06


def tile_layout(tile_count, last_fill, total_tiles, tile_len):
    starts = jnp.cumsum(tile_count) - tile_count
    last_tile = starts + tile_count - 1
    tile_fill = jnp.full((total_tiles,), tile_len, jnp.int32).at[last_tile].set(last_fill)
    return (starts, tile_fill)


def decode(picked, residual_codes, bucket_weights):
    residual = jnp.zeros(residual_codes.shape, jnp.float32)
    for bucket in range(4):
        residual = residual + jnp.where(
            residual_codes == bucket, bucket_weights[bucket][None, :], jnp.float32(0.0)
        )
    summed = picked.astype(jnp.float32) + residual
    scale = lax.rsqrt(jnp.sum(summed * summed, axis=1, keepdims=True) + epsilon)
    return (summed * scale).astype(jnp.bfloat16)


def assemble(own_maxima, candidates, starts, total_tiles, query_len):
    num_queries, num_cand = candidates.shape
    marker = jnp.zeros((total_tiles,), jnp.int32).at[starts].add(1)
    owner_id = jnp.cumsum(marker)
    same_next = jnp.concatenate([owner_id[1:] == owner_id[:-1], jnp.zeros((1,), bool)])
    same_after = jnp.concatenate([owner_id[2:] == owner_id[:-2], jnp.zeros((2,), bool)])
    shifted_one = jnp.concatenate([own_maxima[:, 1:], own_maxima[:, :1]], axis=1)
    shifted_two = jnp.concatenate([own_maxima[:, 2:], own_maxima[:, :2]], axis=1)
    combined = jnp.maximum(own_maxima, jnp.where(same_next[None, :], shifted_one, own_maxima))
    combined = jnp.maximum(combined, jnp.where(same_after[None, :], shifted_two, own_maxima))
    combined = combined.reshape(num_queries, query_len, total_tiles)
    first_tile = starts[candidates]
    selector = (
        first_tile[:, :, None] == jnp.arange(total_tiles, dtype=jnp.int32)[None, None, :]
    ).astype(jnp.float32)
    return jnp.einsum(
        "qit,qct->qc",
        combined,
        selector,
        precision=lax.Precision.HIGHEST,
        preferred_element_type=jnp.float32,
    )


def per_device(
    queries,
    candidates,
    centroids,
    bucket_weights,
    centroid_shard,
    centroid_row,
    residual_codes,
    tile_count,
    last_fill,
):
    n_psg = lax.axis_size("psg")
    shard_index = lax.axis_index("psg")
    tok_dev = residual_codes.shape[0]
    tiles_dev = tok_dev // TILE
    cent_dev = centroids.shape[0]
    owners = centroid_shard[:, 0]
    codebook = lax.all_gather(centroids, "psg", axis=0, tiled=True)
    picked = jnp.take(codebook, owners * cent_dev + centroid_row, axis=0)
    embedded = decode(picked, residual_codes, bucket_weights)
    total_tiles = tiles_dev * n_psg
    starts, tile_fill = tile_layout(tile_count, last_fill, total_tiles, TILE)
    local_fill = lax.dynamic_slice_in_dim(tile_fill, shard_index * tiles_dev, tiles_dev, 0)
    token_mask = jnp.arange(TILE, dtype=jnp.int32)[None, :] < local_fill[:, None]
    pad_bias = jnp.where(token_mask, jnp.float32(0.0), -jnp.inf).reshape(-1)
    per_block = max(1, 512 // TILE)
    while tiles_dev % per_block:
        per_block -= 1
    width = per_block * TILE
    piece = lax.all_gather(queries, "psg", axis=0, tiled=True)
    flat_rows = piece.reshape(-1, piece.shape[-1])
    pieces = []
    for block in range(tiles_dev // per_block):
        key_block = embedded[block * width : (block + 1) * width]
        block_scores = jnp.einsum(
            "qd,kd->qk", flat_rows, key_block, preferred_element_type=jnp.float32
        )
        block_scores = block_scores + pad_bias[block * width : (block + 1) * width][None, :]
        pieces.append(jnp.max(block_scores.reshape(flat_rows.shape[0], per_block, TILE), axis=2))
    maxima = jnp.concatenate(pieces, axis=1)
    own_maxima = lax.all_to_all(maxima, "psg", split_axis=0, concat_axis=1, tiled=True)
    return assemble(own_maxima, candidates, starts, total_tiles, queries.shape[1])


def solution(mesh):
    placed = (
        P(("groups", "psg"), None, None),
        P(("groups", "psg"), None),
        P("psg", None),
        P(),
        P("psg", None),
        P("psg"),
        P("psg", None),
        P(),
        P(),
    )
    return jax.shard_map(
        per_device,
        mesh=mesh,
        in_specs=placed,
        out_specs=P(("groups", "psg"), None),
        check_vma=False,
    )
```

profile of v0, /device:TPU:0, one launch (start us, length us, event | category | flops | bytes accessed | tf_op | source)
XLA Modules:
  0.0 90.6 jit_solution(17494278856567617430)
XLA Ops:
  6.5 0.7 all-gather.2.cloned.1.call-update
  7.3 0.7 pad_bitcast_fusion
  7.9 0.3 reduce-window.16
  8.3 0.1 slice.84
  8.4 0.1 slice_reduce_fusion.1
  8.5 0.1 add_bitcast_fusion.1
  8.6 0.7 compare_select_fusion.2
  9.2 1.7 %scatter_custom_fusion.1 = s32[256]{0:T(256)S(1)} fusion(s32[160]{0:T(256)S(1)} %get-tuple-element.5, s32[160]{0:T(256)S(1)} %broadcast.58, s32[]{:T(128)} %constant.21.clone.1), kind=kCustom, calls=%fused_computation.54 | custom fusion | flops 160 | bytes 1028 | tf_op jit(solution)/shard_map/scatter-add | solution.py:30
  10.9 0.3 reduce-window.24
  11.2 0.1 slice.93
  11.3 0.7 fusion.9
  12.0 1.2 %scatter_custom_fusion = s32[256]{0:T(256)S(1)} fusion(s32[160]{0:T(256)S(1)} %get-tuple-element.17, s32[160]{0:T(256)} %param.17, s32[]{:T(128)} %constant.15.clone.1), kind=kCustom, calls=%fused_computation.56 | custom fusion | bytes 1536 | tf_op jit(solution)/shard_map/scatter | solution.py:13
  13.3 0.1 dynamic_slice.3
  13.4 0.1 slice_reduce_fusion
  13.5 24.3 %all_gather.7 = bf16[32,32,128]{2,1,0:T(8,128)(2,1)S(1)} all-gather(bf16[2,32,128]{2,1,0:T(8,128)(2,1)} %param.9), channel_id=1, replica_groups=mesh['groups'=2,'psg'=16] {'psg'}, dimensions={0}, use_global_device_ids=true | all-gather | bytes 278528 | tf_op jit(solution)/shard_map/all_gather | solution.py:81
  37.9 0.1 slice_compare_fusion
  38.0 0.8 slice_bitcast_fusion.7
  38.9 0.7 broadcast_multiply_fusion
  39.6 0.7 compare_and_fusion
  40.3 0.7 broadcast_clamp_fusion
  41.0 13.0 %all-gather.2.cloned.1.call-done = bf16[8192,128]{1,0:T(8,128)(2,1)} async-done(((bf16[512,128]{1,0:T(8,128)(2,1)}), bf16[8192,128]{1,0:T(8,128)(2,1)}) %all-gather.2.cloned.1.call-update) | async-done | bytes 2097168 | tf_op jit(solution)/shard_map/all_gather | solution.py:69
  54.0 7.5 %gather_fusion = bf16[2048,128]{1,0:T(8,128)(2,1)S(1)} fusion(bf16[8192,128]{1,0:T(8,128)(2,1)} %all-gather.2.cloned.1.call-done, s32[2048]{0:T(1024)S(1)} %broadcast_clamp_fusion), kind=kCustom, calls=%fused_computation | custom fusion | bytes 1056768 | tf_op jit(solution)/shard_map/jit(_take)/gather | solution.py:70
  61.5 0.9 multiply_reduce_fusion
  62.4 0.3 multiply_convert_fusion
  62.8 0.5 bitcast_reduce_fusion.3
  63.2 0.5 bitcast_reduce_fusion.2
  63.7 0.5 bitcast_reduce_fusion.1
  64.2 0.5 bitcast_reduce_fusion
  64.6 0.1 all_to_all.16
  64.8 0.7 reshape.153
  65.5 3.5 %all-to-all-start = ((f32[16,1,1024]{2,1,0:T(1,128)}), f32[16,1,1024]{2,1,0:T(1,128)S(1)}, u32[]{:S(2)}, u32[]{:S(2)}) async-start(f32[16,1,1024]{2,1,0:T(1,128)} %reshape.153), calls=%async_computation | async-start | bytes 131072 | tf_op jit(solution)/shard_map/all_to_all | solution.py:92
  69.0 0.1 slice_compare_fusion.1
  69.1 6.8 %gather_fusion.1 = s32[1024]{0:T(1024)S(1)} fusion(s32[160]{0:T(256)S(1)} %get-tuple-element.6, s32[1024]{0:T(1024)S(1)} %broadcast_clamp_fusion.1), kind=kCustom, calls=%fused_computation.1 | custom fusion | bytes 12288 | tf_op jit(solution)/shard_map/gather | solution.py:39
  76.0 0.1 pad_add_fusion
  76.0 0.5 broadcast.78
  76.6 0.8 reduce.8
  77.4 0.1 reshape.154
  77.5 0.1 copy.28
  77.6 0.2 copy.29
  77.8 0.1 copy.30
  77.9 0.2 copy.31
  78.0 0.2 all_to_all.19
  78.2 0.1 concatenate.32
  78.3 0.1 concatenate.28
  78.4 4.0 %fusion.3 = f32[2,256]{0,1:T(8,128)S(1)} fusion(f32[2,32,256]{1,0,2:T(2,128)S(1)} %all_to_all.19, f32[2,32,1]{1,0,2:T(2,128)S(1)} %concatenate.28, f32[2,32,255]{1,0,2:T(2,128)S(1)} %copy.29, f32[2,32,2]{1,0,2:T(2,128)S(1)} %concatenate.32, f32[2,32,254]{1,0,2:T(2,128)S(1)} %copy.31, pred[256]{0:T(512)(128)(4,1)S(1)} %concatenate.30, ...), kind=kLoop, calls=%fused_computation.20 | loop fusion | flops 114176 | bytes 199168 | tf_op jit(solution)/shard_map/qit,qct->qc/reduce_sum | solution.py:43
  82.4 0.1 copy.32
  82.5 0.6 fusion
  83.1 0.6 copy.37
  (22 shorter events, 0.4 us)
Async XLA Ops:
  6.5 47.5 %all-gather.2.cloned.1.call-start = ((), (), s32[]{:S(2)}) async-start(), calls=%async_computation.1 | async-start | bytes 2228224 | tf_op jit(solution)/shard_map/all_gather | solution.py:69
  41.0 20.5 %copy-start = (s32[2048,128]{1,0:T(8,128)S(1)}, s32[2048,128]{1,0:T(8,128)}, u32[]{:S(2)}) copy-start(s32[2048,128]{1,0:T(8,128)} %param.15) | copy-start | bytes 3145732
  65.5 10.5 %all-to-all-start = ((f32[16,1,1024]{2,1,0:T(1,128)}), f32[16,1,1024]{2,1,0:T(1,128)S(1)}, u32[]{:S(2)}, u32[]{:S(2)}) async-start(f32[16,1,1024]{2,1,0:T(1,128)} %reshape.153), calls=%async_computation | async-start | bytes 131072 | tf_op jit(solution)/shard_map/all_to_all | solution.py:92
Sparse Core Ops, SparseCore 0:
  9.5 44.4 all-gather.1
where the time goes:
time: 91.1 us; the launch traced here: 90.6 us
  blocking collectives  24.3 us (27%)
  local copies, waits for them, and re-layouts  20.6 us (23%)
  waiting for transfers between devices  13.8 us (15%)
  between operations  13.6 us (15%)
  other arithmetic  12.4 us (14%)
  starting transfers between devices  3.5 us (4%)
  matrix products  2.45 us (3%)
    all_gather x1, blocking collectives, per_device(): piece = lax.all_gather(queries, 'psg', axis=0, tiled=True)  24.3 us
    all_gather x1, waiting for transfers between devices, per_device(): codebook = lax.all_gather(centroids, 'psg', axis=0, tiled=True)  13 us
    gather x1, local copies, waits for them, and re-layouts, per_device(): picked = jnp.take(codebook, owners * cent_dev + centroid_row, axis=0)  7.45 us
    gather x2, local copies, waits for them, and re-layouts, assemble(): first_tile = starts[candidates]  6.83 us
    reduce_sum x1, other arithmetic, assemble(): jnp.einsum('qit,qct->qc', combined, selector, precision=lax.Precision.HIG...  4.02 us
    all_to_all x1, starting transfers between devices, per_device(): lax.all_to_all(maxima, 'psg', split_axis=0, concat_axis=1, tiled=True)  3.5 us
    dot_general x4, matrix products, per_device(): jnp.einsum('qd,kd->qk', flat_rows, key_block, preferred_element_type=jnp....  1.83 us
  transfers between devices with their start and end apart: 2, of which 1 were waited for; matrix products, arithmetic and copies ran while one was open for 18% of the time, Pallas kernels for 0%

commit v1 on v0

--- a/solution.py
+++ b/solution.py
@@ -89,7 +89,19 @@
         block_scores = block_scores + pad_bias[block * width : (block + 1) * width][None, :]
         pieces.append(jnp.max(block_scores.reshape(flat_rows.shape[0], per_block, TILE), axis=2))
     maxima = jnp.concatenate(pieces, axis=1)
-    own_maxima = lax.all_to_all(maxima, "psg", split_axis=0, concat_axis=1, tiled=True)
+    ways, here = (lax.axis_size("psg"), lax.axis_index("psg"))
+    width_2 = maxima.shape[0] // ways
+    shape = list(maxima.shape)
+    shape[0] = width_2
+    height = shape[1]
+    shape[1] = height * ways
+    full = jnp.zeros(shape, maxima.dtype)
+    for mask in range(ways):
+        part = lax.dynamic_slice_in_dim(maxima, (here ^ mask) * width_2, width_2, axis=0)
+        if mask:
+            part = lax.ppermute(part, "psg", [(d, d ^ mask) for d in range(ways)])
+        full = lax.dynamic_update_slice_in_dim(full, part, (here ^ mask) * height, axis=1)
+    own_maxima = full
     return assemble(own_maxima, candidates, starts, total_tiles, queries.shape[1])
 
 

time: 91.1 us -> 111 us (1.22)
  starting transfers between devices: 3.5 us -> 20.7 us
  local copies, waits for them, and re-layouts: 20.6 us -> 27.9 us
  other arithmetic: 12.4 us -> 7.66 us
    ppermute x0 -> x15, starting transfers between devices: none -> 20.7 us  [per_device(): part = lax.ppermute(part, 'psg', [(d, d ^ mask) for d in range(ways)])]
    dynamic_update_slice x0 -> x16, local copies, waits for them, and re-layouts: none -> 8.1 us  [per_device(): lax.dynamic_update_slice_in_dim(full, part, (here ^ mask) * height, axis=1)]
    reduce_sum x1, other arithmetic: 4.02 us -> 0.11 us  [assemble(): jnp.einsum('qit,qct->qc', combined, selector, precision=lax.Precision.HIG...]
    all_to_all x1 -> x0, starting transfers between devices: 3.5 us -> none  [per_device(): lax.all_to_all(maxima, 'psg', split_axis=0, concat_axis=1, tiled=True)]
  transfers between devices with their start and end apart: 2 -> 16, of which waited for: 1 -> 1; matrix products, arithmetic and copies ran while one was open for 18% -> 23% of each run, Pallas kernels for 0% -> 0%
where the time goes in v1:
time: 111 us
  local copies, waits for them, and re-layouts  27.9 us (25%)
  blocking collectives  24.4 us (22%)
  starting transfers between devices  20.7 us (19%)
  between operations  13.9 us (13%)
  waiting for transfers between devices  13.7 us (12%)
  other arithmetic  7.66 us (7%)
  matrix products  2.45 us (2%)
    all_gather x1, blocking collectives, per_device(): piece = lax.all_gather(queries, 'psg', axis=0, tiled=True)  24.4 us
    ppermute x15, starting transfers between devices, per_device(): part = lax.ppermute(part, 'psg', [(d, d ^ mask) for d in range(ways)])  20.7 us
    all_gather x1, waiting for transfers between devices, per_device(): codebook = lax.all_gather(centroids, 'psg', axis=0, tiled=True)  12.9 us
    dynamic_update_slice x16, local copies, waits for them, and re-layouts, per_device(): lax.dynamic_update_slice_in_dim(full, part, (here ^ mask) * height, axis=1)  8.1 us
    gather x1, local copies, waits for them, and re-layouts, per_device(): picked = jnp.take(codebook, owners * cent_dev + centroid_row, axis=0)  7.45 us
    gather x2, local copies, waits for them, and re-layouts, assemble(): first_tile = starts[candidates]  6.83 us
  transfers between devices with their start and end apart: 16, of which 1 were waited for; matrix products, arithmetic and copies ran while one was open for 23% of the time, Pallas kernels for 0%

profile of v1, /device:TPU:0, one launch (start us, length us, event | category | flops | bytes accessed | tf_op | source)
XLA Modules:
  0.0 110.7 jit_solution(1458139376438223248)
XLA Ops:
  6.5 0.7 all-gather.2.cloned.1.call-update
  7.3 0.7 pad_bitcast_fusion
  8.6 0.7 compare_select_fusion.2
  9.3 1.7 %scatter_custom_fusion.1 = s32[256]{0:T(256)S(1)} fusion(s32[160]{0:T(256)S(1)} %get-tuple-element.5, s32[160]{0:T(256)S(1)} %broadcast.50, s32[]{:T(128)} %constant.36.clone.1), kind=kCustom, calls=%fused_computation.70 | custom fusion | flops 160 | bytes 1028 | tf_op jit(solution)/shard_map/scatter-add | solution.py:30
  11.4 0.7 fusion.8
  12.1 1.2 %scatter_custom_fusion = s32[256]{0:T(256)S(1)} fusion(s32[160]{0:T(256)S(1)} %get-tuple-element.33, s32[160]{0:T(256)} %param.17, s32[]{:T(128)} %constant.44.clone.1), kind=kCustom, calls=%fused_computation.72 | custom fusion | bytes 1536 | tf_op jit(solution)/shard_map/scatter | solution.py:13
  13.6 24.4 %all_gather.7 = bf16[32,32,128]{2,1,0:T(8,128)(2,1)S(1)} all-gather(bf16[2,32,128]{2,1,0:T(8,128)(2,1)} %param.9), channel_id=1, replica_groups=mesh['groups'=2,'psg'=16] {'psg'}, dimensions={0}, use_global_device_ids=true | all-gather | bytes 278528 | tf_op jit(solution)/shard_map/all_gather | solution.py:81
  38.1 0.8 slice_bitcast_fusion.7
  39.1 0.7 broadcast_multiply_fusion
  39.8 0.7 compare_and_fusion
  40.5 0.7 broadcast_clamp_fusion
  41.2 12.9 %all-gather.2.cloned.1.call-done = bf16[8192,128]{1,0:T(8,128)(2,1)} async-done(((bf16[512,128]{1,0:T(8,128)(2,1)}), bf16[8192,128]{1,0:T(8,128)(2,1)}) %all-gather.2.cloned.1.call-update) | async-done | bytes 2097168 | tf_op jit(solution)/shard_map/all_gather | solution.py:69
  54.1 7.5 %gather_fusion = bf16[2048,128]{1,0:T(8,128)(2,1)S(1)} fusion(bf16[8192,128]{1,0:T(8,128)(2,1)} %all-gather.2.cloned.1.call-done, s32[2048]{0:T(1024)S(1)} %broadcast_clamp_fusion), kind=kCustom, calls=%fused_computation | custom fusion | bytes 1056768 | tf_op jit(solution)/shard_map/jit(_take)/gather | solution.py:70
  61.6 0.9 multiply_reduce_fusion
  62.8 0.5 bitcast_reduce_fusion.3
  63.3 0.5 bitcast_reduce_fusion.2
  63.8 0.5 bitcast_reduce_fusion.1
  64.2 0.5 bitcast_reduce_fusion
  65.3 0.6 collective-permute-start.1
  66.0 1.1 collective-permute-start.2
  67.6 1.6 %collective-permute-start.4 = (f32[64,16]{1,0:T(8,128)S(1)}, f32[64,16]{1,0:T(8,128)S(1)}, u32[]{:S(2)}, u32[]{:S(2)}) collective-permute-start(f32[64,16]{1,0:T(8,128)S(1)} %copy.33), channel_id=1, source_target_pairs={{0,5},{1,4},{2,7},{3,6},{4,1},{5,0},{6,3},{7,2},{8,13},{9,12},{10,... | collective-permute-start | bytes 12296 | tf_op jit(solution)/shard_map/ppermute | solution.py:102
  69.7 0.5 collective-permute-start.5
  70.2 2.1 %collective-permute-start.6 = (f32[64,16]{1,0:T(8,128)S(1)}, f32[64,16]{1,0:T(8,128)S(1)}, u32[]{:S(2)}, u32[]{:S(2)}) collective-permute-start(f32[64,16]{1,0:T(8,128)S(1)} %copy.35), channel_id=1, source_target_pairs={{0,7},{1,6},{2,5},{3,4},{4,3},{5,2},{6,1},{7,0},{8,15},{9,14},{10,... | collective-permute-start | bytes 12296 | tf_op jit(solution)/shard_map/ppermute | solution.py:102
  72.3 0.7 collective-permute-start.7
  73.0 2.1 %collective-permute-start.8 = (f32[64,16]{1,0:T(8,128)S(1)}, f32[64,16]{1,0:T(8,128)S(1)}, u32[]{:S(2)}, u32[]{:S(2)}) collective-permute-start(f32[64,16]{1,0:T(8,128)S(1)} %copy.37), channel_id=1, source_target_pairs={{0,9},{1,8},{2,11},{3,10},{4,13},{5,12},{6,15},{7,14},{8,1},{9,0},... | collective-permute-start | bytes 12296 | tf_op jit(solution)/shard_map/ppermute | solution.py:102
  75.0 0.9 collective-permute-start.9
  76.4 2.6 %collective-permute-start.10 = (f32[64,16]{1,0:T(8,128)S(1)}, f32[64,16]{1,0:T(8,128)S(1)}, u32[]{:S(2)}, u32[]{:S(2)}) collective-permute-start(f32[64,16]{1,0:T(8,128)S(1)} %copy.39), channel_id=1, source_target_pairs={{0,11},{1,10},{2,9},{3,8},{4,15},{5,14},{6,13},{7,12},{8,3},{9,2},... | collective-permute-start | bytes 12296 | tf_op jit(solution)/shard_map/ppermute | solution.py:102
  79.0 2.1 %collective-permute-start.11 = (f32[64,16]{1,0:T(8,128)S(1)}, f32[64,16]{1,0:T(8,128)S(1)}, u32[]{:S(2)}, u32[]{:S(2)}) collective-permute-start(f32[64,16]{1,0:T(8,128)S(1)} %copy.40), channel_id=1, source_target_pairs={{0,12},{1,13},{2,14},{3,15},{4,8},{5,9},{6,10},{7,11},{8,4},{9,5},... | collective-permute-start | bytes 12296 | tf_op jit(solution)/shard_map/ppermute | solution.py:102
  81.1 1.6 %collective-permute-start.12 = (f32[64,16]{1,0:T(8,128)S(1)}, f32[64,16]{1,0:T(8,128)S(1)}, u32[]{:S(2)}, u32[]{:S(2)}) collective-permute-start(f32[64,16]{1,0:T(8,128)S(1)} %copy.41), channel_id=1, source_target_pairs={{0,13},{1,12},{2,15},{3,14},{4,9},{5,8},{6,11},{7,10},{8,5},{9,4},... | collective-permute-start | bytes 12296 | tf_op jit(solution)/shard_map/ppermute | solution.py:102
  82.7 2.0 %collective-permute-start.13 = (f32[64,16]{1,0:T(8,128)S(1)}, f32[64,16]{1,0:T(8,128)S(1)}, u32[]{:S(2)}, u32[]{:S(2)}) collective-permute-start(f32[64,16]{1,0:T(8,128)S(1)} %copy.42), channel_id=1, source_target_pairs={{0,14},{1,15},{2,12},{3,13},{4,10},{5,11},{6,8},{7,9},{8,6},{9,7},... | collective-permute-start | bytes 12296 | tf_op jit(solution)/shard_map/ppermute | solution.py:102
  84.7 2.3 %collective-permute-start.14 = (f32[64,16]{1,0:T(8,128)S(1)}, f32[64,16]{1,0:T(8,128)S(1)}, u32[]{:S(2)}, u32[]{:S(2)}) collective-permute-start(f32[64,16]{1,0:T(8,128)S(1)} %copy.43), channel_id=1, source_target_pairs={{0,15},{1,14},{2,13},{3,12},{4,11},{5,10},{6,9},{7,8},{8,7},{9,6},... | collective-permute-start | bytes 12296 | tf_op jit(solution)/shard_map/ppermute | solution.py:102
  87.0 6.8 %gather_fusion.1 = s32[1024]{0:T(1024)S(1)} fusion(s32[160]{0:T(256)S(1)} %get-tuple-element.6, s32[1024]{0:T(1024)S(1)} %broadcast_clamp_fusion.1), kind=kCustom, calls=%fused_computation.1 | custom fusion | bytes 12288 | tf_op jit(solution)/shard_map/gather | solution.py:39
  94.5 0.6 dynamic_update_slice.49
  95.1 0.6 dynamic_update_slice.50
  95.7 0.6 dynamic_update_slice.51
  96.3 0.6 dynamic_update_slice.52
  96.9 0.6 dynamic_update_slice.53
  97.5 0.6 dynamic_update_slice.54
  98.1 0.6 dynamic_update_slice.55
  99.0 0.5 dynamic_update_slice.57
  99.5 0.5 dynamic_update_slice.58
  100.0 0.5 dynamic_update_slice.59
  100.5 0.5 dynamic_update_slice.60
  100.9 0.5 dynamic_update_slice.61
  101.4 0.5 dynamic_update_slice.62
  101.9 0.5 dynamic_update_slice.63
  102.6 0.6 fusion
  103.2 0.6 copy.48
  (69 shorter events, 5.2 us)
Async XLA Ops:
  6.5 47.6 %all-gather.2.cloned.1.call-start = ((), (), s32[]{:S(2)}) async-start(), calls=%async_computation | async-start | bytes 2228224 | tf_op jit(solution)/shard_map/all_gather | solution.py:69
  41.2 20.4 %copy-start = (s32[2048,128]{1,0:T(8,128)S(1)}, s32[2048,128]{1,0:T(8,128)}, u32[]{:S(2)}) copy-start(s32[2048,128]{1,0:T(8,128)} %param.15) | copy-start | bytes 3145732
  65.0 4.7 %collective-permute-start = (f32[64,16]{1,0:T(8,128)S(1)}, f32[64,16]{1,0:T(8,128)S(1)}, u32[]{:S(2)}, u32[]{:S(2)}) collective-permute-start(f32[64,16]{1,0:T(8,128)S(1)} %copy.29), channel_id=1, source_target_pairs={{0,1},{1,0},{2,3},{3,2},{4,5},{5,4},{6,7},{7,6},{8,9},{9,8},{10,11... | collective-permute-start | bytes 12296 | tf_op jit(solution)/shard_map/ppermute | solution.py:102
  65.3 4.8 %collective-permute-start.1 = (f32[64,16]{1,0:T(8,128)S(1)}, f32[64,16]{1,0:T(8,128)S(1)}, u32[]{:S(2)}, u32[]{:S(2)}) collective-permute-start(f32[64,16]{1,0:T(8,128)S(1)} %copy.30), channel_id=1, source_target_pairs={{0,2},{1,3},{2,0},{3,1},{4,6},{5,7},{6,4},{7,5},{8,10},{9,11},{10,... | collective-permute-start | bytes 12296 | tf_op jit(solution)/shard_map/ppermute | solution.py:102
  66.0 6.3 %collective-permute-start.2 = (f32[64,16]{1,0:T(8,128)S(1)}, f32[64,16]{1,0:T(8,128)S(1)}, u32[]{:S(2)}, u32[]{:S(2)}) collective-permute-start(f32[64,16]{1,0:T(8,128)S(1)} %copy.31), channel_id=1, source_target_pairs={{0,3},{1,2},{2,1},{3,0},{4,7},{5,6},{6,5},{7,4},{8,11},{9,10},{10,... | collective-permute-start | bytes 12296 | tf_op jit(solution)/shard_map/ppermute | solution.py:102
  67.2 5.8 %collective-permute-start.3 = (f32[64,16]{1,0:T(8,128)S(1)}, f32[64,16]{1,0:T(8,128)S(1)}, u32[]{:S(2)}, u32[]{:S(2)}) collective-permute-start(f32[64,16]{1,0:T(8,128)S(1)} %copy.32), channel_id=1, source_target_pairs={{0,4},{1,5},{2,6},{3,7},{4,0},{5,1},{6,2},{7,3},{8,12},{9,13},{10,... | collective-permute-start | bytes 12296 | tf_op jit(solution)/shard_map/ppermute | solution.py:102
  67.6 7.4 %collective-permute-start.4 = (f32[64,16]{1,0:T(8,128)S(1)}, f32[64,16]{1,0:T(8,128)S(1)}, u32[]{:S(2)}, u32[]{:S(2)}) collective-permute-start(f32[64,16]{1,0:T(8,128)S(1)} %copy.33), channel_id=1, source_target_pairs={{0,5},{1,4},{2,7},{3,6},{4,1},{5,0},{6,3},{7,2},{8,13},{9,12},{10,... | collective-permute-start | bytes 12296 | tf_op jit(solution)/shard_map/ppermute | solution.py:102
  69.7 6.7 %collective-permute-start.5 = (f32[64,16]{1,0:T(8,128)S(1)}, f32[64,16]{1,0:T(8,128)S(1)}, u32[]{:S(2)}, u32[]{:S(2)}) collective-permute-start(f32[64,16]{1,0:T(8,128)S(1)} %copy.34), channel_id=1, source_target_pairs={{0,6},{1,7},{2,4},{3,5},{4,2},{5,3},{6,0},{7,1},{8,14},{9,15},{10,... | collective-permute-start | bytes 12296 | tf_op jit(solution)/shard_map/ppermute | solution.py:102
  70.2 8.9 %collective-permute-start.6 = (f32[64,16]{1,0:T(8,128)S(1)}, f32[64,16]{1,0:T(8,128)S(1)}, u32[]{:S(2)}, u32[]{:S(2)}) collective-permute-start(f32[64,16]{1,0:T(8,128)S(1)} %copy.35), channel_id=1, source_target_pairs={{0,7},{1,6},{2,5},{3,4},{4,3},{5,2},{6,1},{7,0},{8,15},{9,14},{10,... | collective-permute-start | bytes 12296 | tf_op jit(solution)/shard_map/ppermute | solution.py:102
  72.3 8.8 %collective-permute-start.7 = (f32[64,16]{1,0:T(8,128)S(1)}, f32[64,16]{1,0:T(8,128)S(1)}, u32[]{:S(2)}, u32[]{:S(2)}) collective-permute-start(f32[64,16]{1,0:T(8,128)S(1)} %copy.36), channel_id=1, source_target_pairs={{0,8},{1,9},{2,10},{3,11},{4,12},{5,13},{6,14},{7,15},{8,0},{9,1},... | collective-permute-start | bytes 12296 | tf_op jit(solution)/shard_map/ppermute | solution.py:102
  73.0 9.7 %collective-permute-start.8 = (f32[64,16]{1,0:T(8,128)S(1)}, f32[64,16]{1,0:T(8,128)S(1)}, u32[]{:S(2)}, u32[]{:S(2)}) collective-permute-start(f32[64,16]{1,0:T(8,128)S(1)} %copy.37), channel_id=1, source_target_pairs={{0,9},{1,8},{2,11},{3,10},{4,13},{5,12},{6,15},{7,14},{8,1},{9,0},... | collective-permute-start | bytes 12296 | tf_op jit(solution)/shard_map/ppermute | solution.py:102
  75.0 9.7 %collective-permute-start.9 = (f32[64,16]{1,0:T(8,128)S(1)}, f32[64,16]{1,0:T(8,128)S(1)}, u32[]{:S(2)}, u32[]{:S(2)}) collective-permute-start(f32[64,16]{1,0:T(8,128)S(1)} %copy.38), channel_id=1, source_target_pairs={{0,10},{1,11},{2,8},{3,9},{4,14},{5,15},{6,12},{7,13},{8,2},{9,3},... | collective-permute-start | bytes 12296 | tf_op jit(solution)/shard_map/ppermute | solution.py:102
  76.4 23.6 %collective-permute-start.10 = (f32[64,16]{1,0:T(8,128)S(1)}, f32[64,16]{1,0:T(8,128)S(1)}, u32[]{:S(2)}, u32[]{:S(2)}) collective-permute-start(f32[64,16]{1,0:T(8,128)S(1)} %copy.39), channel_id=1, source_target_pairs={{0,11},{1,10},{2,9},{3,8},{4,15},{5,14},{6,13},{7,12},{8,3},{9,2},... | collective-permute-start | bytes 12296 | tf_op jit(solution)/shard_map/ppermute | solution.py:102
  79.0 21.4 %collective-permute-start.11 = (f32[64,16]{1,0:T(8,128)S(1)}, f32[64,16]{1,0:T(8,128)S(1)}, u32[]{:S(2)}, u32[]{:S(2)}) collective-permute-start(f32[64,16]{1,0:T(8,128)S(1)} %copy.40), channel_id=1, source_target_pairs={{0,12},{1,13},{2,14},{3,15},{4,8},{5,9},{6,10},{7,11},{8,4},{9,5},... | collective-permute-start | bytes 12296 | tf_op jit(solution)/shard_map/ppermute | solution.py:102
  81.1 19.8 %collective-permute-start.12 = (f32[64,16]{1,0:T(8,128)S(1)}, f32[64,16]{1,0:T(8,128)S(1)}, u32[]{:S(2)}, u32[]{:S(2)}) collective-permute-start(f32[64,16]{1,0:T(8,128)S(1)} %copy.41), channel_id=1, source_target_pairs={{0,13},{1,12},{2,15},{3,14},{4,9},{5,8},{6,11},{7,10},{8,5},{9,4},... | collective-permute-start | bytes 12296 | tf_op jit(solution)/shard_map/ppermute | solution.py:102
  82.7 18.7 %collective-permute-start.13 = (f32[64,16]{1,0:T(8,128)S(1)}, f32[64,16]{1,0:T(8,128)S(1)}, u32[]{:S(2)}, u32[]{:S(2)}) collective-permute-start(f32[64,16]{1,0:T(8,128)S(1)} %copy.42), channel_id=1, source_target_pairs={{0,14},{1,15},{2,12},{3,13},{4,10},{5,11},{6,8},{7,9},{8,6},{9,7},... | collective-permute-start | bytes 12296 | tf_op jit(solution)/shard_map/ppermute | solution.py:102
  84.7 17.1 %collective-permute-start.14 = (f32[64,16]{1,0:T(8,128)S(1)}, f32[64,16]{1,0:T(8,128)S(1)}, u32[]{:S(2)}, u32[]{:S(2)}) collective-permute-start(f32[64,16]{1,0:T(8,128)S(1)} %copy.43), channel_id=1, source_target_pairs={{0,15},{1,14},{2,13},{3,12},{4,11},{5,10},{6,9},{7,8},{8,7},{9,6},... | collective-permute-start | bytes 12296 | tf_op jit(solution)/shard_map/ppermute | solution.py:102
Sparse Core Ops, SparseCore 0:
  9.5 44.5 all-gather.1
